TPU v7x, 32 devices: a whole 2x2x4 slice. The times are simulated.
32 devices in a mesh: row: 16 (over z, x, core), col: 2 (over y).
Axes of the slice: x: 2, y: 2, z: 4, core: 2. Of those that a mesh axis runs over, the one named last changes fastest.
Arguments:
- token_ids: int32 [512], P('col'), may hold values from 0 to 50559, as said below
- table: bfloat16 [50560, 5120], P('row', 'col'), may hold values from -120 to 120
- norm_gain: float32 [5120], replicated, may hold values from 0.5 to 1.5
- w_qkv: bfloat16 [5120, 7168], P('col', 'row'), may hold values from -0.078125 to 0.078125
- w_gate: bfloat16 [5120, 16384], P('col', 'row'), may hold values from -0.078125 to 0.078125
- w_up: bfloat16 [5120, 16384], P('col', 'row'), may hold values from -0.078125 to 0.078125
Outputs:
- qkv_out: bfloat16 [512, 7168], P('col', 'row')
- hidden: bfloat16 [512, 16384], P('col', 'row')
Inputs may be any that keep to these rules, and one draw needn't show every extreme that they name: `token_ids`: most ids of the micro-batch lie in one block of 3160 entries that starts at a multiple of 3160, which block being drawn; the others lie in the other blocks.
All inputs are finite; a program needn't handle non-finite values.
Results may differ from a plain program's by a relative error of at most 0.0058.
Values may be sent and summed in bfloat16 or wider, within the bound.
A program may use at most 128 MiB of HBM per device.

v0:
```python
import math

import jax
import jax.numpy as jnp
from jax import lax
from jax.sharding import PartitionSpec as P

eps = 1e-05


def lookup_partial(every_id, table_tile, vocab_first):
    total_rows = every_id.shape[0]
    block_rows = math.gcd(total_rows, 512)
    columns = vocab_first + lax.broadcasted_iota(jnp.int32, (1, table_tile.shape[0]), 1)

    def one_block(block_ids):
        onehot = (block_ids[:, None] == columns).astype(jnp.bfloat16)
        return jnp.dot(onehot, table_tile, preferred_element_type=jnp.float32).astype(jnp.bfloat16)

    pieces_out = lax.map(one_block, every_id.reshape(total_rows // block_rows, block_rows))
    return pieces_out.reshape(total_rows, table_tile.shape[1])


def body(token_ids, table, norm_gain, w_qkv, w_gate, w_up):
    every_id = lax.all_gather(token_ids, "col", axis=0, tiled=True)
    vocab_rows = table.shape[0]
    partial_value = lookup_partial(every_id, table, lax.axis_index("row") * vocab_rows)
    embedded = lax.psum(partial_value, "row").astype(jnp.float32).astype(jnp.bfloat16)
    token_rows = lax.all_to_all(embedded, "col", split_axis=0, concat_axis=1, tiled=True)
    values = token_rows.astype(jnp.float32)
    factor = lax.rsqrt(jnp.mean(values * values, axis=1, keepdims=True) + eps)
    normed = (values * factor * norm_gain[None, :]).astype(jnp.bfloat16)
    pieces = (
        lax.all_gather(w_qkv, "col", axis=0, tiled=True),
        lax.all_gather(w_gate, "col", axis=0, tiled=True),
        lax.all_gather(w_up, "col", axis=0, tiled=True),
    )
    qkv_total, gate_total, up_total = tuple(
        (jnp.dot(normed, piece, preferred_element_type=jnp.float32) for piece in pieces)
    )
    qkv_out = qkv_total.astype(jnp.bfloat16)
    hidden = (jax.nn.silu(gate_total) * up_total).astype(jnp.bfloat16)
    return (qkv_out, hidden)


def solution(mesh):
    return jax.shard_map(
        body,
        mesh=mesh,
        in_specs=(
            P("col"),
            P("row", "col"),
            P(),
            P("col", "row"),
            P("col", "row"),
            P("col", "row"),
        ),
        out_specs=(P("col", "row"), P("col", "row")),
        check_vma=False,
    )
```

profile of v0, /device:TPU:0, one launch (start us, length us, event | category | flops | bytes accessed | tf_op | source)
XLA Modules:
  0.0 398.8 jit_solution(8804500506668590405)
XLA Ops:
  8.0 0.0 all-reduce.2.cloned.1.call-start
  8.1 5.4 %all-gather = s32[2,1,256]{2,1,0:T(1,128)S(1)} all-gather(s32[1,1,256]{2,1,0:T(1,128)} %bitcast.20), channel_id=1, replica_groups=mesh['row'=16,'col'=2] {'col'}, dimensions={0}, use_global_device_ids=true | all-gather | bytes 3072 | tf_op jit(solution)/shard_map/all_gather | solution.py:25
  13.5 12.5 %fusion.4 = bf16[512,2560]{1,0:T(8,128)(2,1)S(1)} fusion(bf16[3160,2560]{1,0:T(8,128)(2,1)} %param.7, s32[3160]{0:T(1024)S(1)} %iota_add_fusion, s32[512]{0:T(512)S(1)} %bitcast.19), kind=kOutput, calls=%fused_computation.6 | convolution fusion | flops 8286679040 | bytes 18815328 | tf_op jit(solution)/shard_map/while/body/eval_jaxpr/dot_general | solution.py:18
  26.1 2.6 copy.9
  28.6 0.0 all-reduce.2.cloned.1.call-update
  28.6 0.0 all-gather.5.cloned.1.call-start
  28.7 0.5 all-gather.5.cloned.1.call-update
  29.2 0.0 all-gather.7.cloned.1.call-start
  29.3 0.5 all-gather.7.cloned.1.call-update
  29.8 0.0 all-gather.9.cloned.1.call-start
  29.9 0.5 all-gather.9.cloned.1.call-update
  30.4 0.0 copy-start
  30.4 100.8 %all-reduce.2.cloned.1.call-done = bf16[2,256,2560]{1,2,0:T(8,128)(2,1)} async-done(((bf16[2,256,2560]{1,2,0:T(8,128)(2,1)}), bf16[2,256,2560]{1,2,0:T(8,128)(2,1)}) %all-reduce.2.cloned.1.call-update) | async-done | bytes 2621456 | tf_op jit(solution)/shard_map/psum | solution.py:28
  131.2 63.0 %all_to_all.13 = bf16[2,256,2560]{1,2,0:T(8,128)(2,1)S(1)} all-to-all(bf16[2,256,2560]{1,2,0:T(8,128)(2,1)} %all-reduce.2.cloned.1.call-done), channel_id=1, replica_groups=mesh['row'=16,'col'=2] {'col'}, dimensions={0} | all-to-all | bytes 5242880 | tf_op jit(solution)/shard_map/all_to_all | solution.py:29
  194.1 0.7 multiply_reduce_fusion
  194.9 0.0 copy-done
  194.9 2.2 fusion.3
  197.1 0.0 all-gather.5.cloned.1.call-done
  197.1 4.3 %convolution_convert_fusion = bf16[256,448]{0,1:T(8,128)(2,1)} fusion(bf16[5120,448]{0,1:T(8,128)(2,1)} %all-gather.5.cloned.1.call-done, bf16[256,5120]{0,1:T(8,128)(2,1)S(1)} %fusion.3), kind=kOutput, calls=%fused_computation.11 | convolution fusion | flops 1174519808 | bytes 7438336 | tf_op jit(solution)/shard_map/dot_general | solution.py:39
  201.4 51.0 %all-gather.7.cloned.1.call-done = bf16[5120,1024]{1,0:T(8,128)(2,1)} async-done(((bf16[2560,1024]{1,0:T(8,128)(2,1)}), bf16[5120,1024]{1,0:T(8,128)(2,1)}) %all-gather.7.cloned.1.call-update) | async-done | bytes 10485776 | tf_op jit(solution)/shard_map/all_gather | solution.py:35
  252.4 7.8 %fusion.10 = f32[256,1024]{1,0:T(8,128)} fusion(bf16[256,5120]{0,1:T(8,128)(2,1)S(1)} %fusion.3, bf16[5120,1024]{1,0:T(8,128)(2,1)} %all-gather.7.cloned.1.call-done), kind=kOutput, calls=%fused_computation.14 | convolution fusion | flops 2684354560 | bytes 14155776 | tf_op jit(solution)/shard_map/dot_general | solution.py:39
  260.2 123.0 %all-gather.9.cloned.1.call-done = bf16[5120,1024]{1,0:T(8,128)(2,1)} async-done(((bf16[2560,1024]{1,0:T(8,128)(2,1)}), bf16[5120,1024]{1,0:T(8,128)(2,1)}) %all-gather.9.cloned.1.call-update) | async-done | bytes 10485776 | tf_op jit(solution)/shard_map/all_gather | solution.py:36
  383.2 8.0 %fusion.9 = bf16[256,1024]{1,0:T(8,128)(2,1)} fusion(bf16[256,5120]{0,1:T(8,128)(2,1)S(1)} %fusion.3, bf16[5120,1024]{1,0:T(8,128)(2,1)} %all-gather.9.cloned.1.call-done, f32[256,1024]{1,0:T(8,128)} %fusion.10), kind=kOutput, calls=%fused_computation.10 | convolution fusion | flops 2685927424 | bytes 14680064 | tf_op jit(solution)/shard_map/dot_general | solution.py:39
  (2 shorter events, 0.0 us)
Async XLA Ops:
  8.0 123.2 %all-reduce.2.cloned.1.call-start = ((), (), s32[]{:S(2)}) async-start(), calls=%async_computation.1 | async-start | bytes 5242880 | tf_op jit(solution)/shard_map/psum | solution.py:28
  28.6 168.4 %all-gather.5.cloned.1.call-start = ((), (), s32[]{:S(2)}) async-start(), calls=%async_computation.2 | async-start | bytes 6881280 | tf_op jit(solution)/shard_map/all_gather | solution.py:34
  29.2 223.2 %all-gather.7.cloned.1.call-start = ((), (), s32[]{:S(2)}) async-start(), calls=%async_computation.3 | async-start | bytes 15728640 | tf_op jit(solution)/shard_map/all_gather | solution.py:35
  29.8 353.4 %all-gather.9.cloned.1.call-start = ((), (), s32[]{:S(2)}) async-start(), calls=%async_computation.4 | async-start | bytes 15728640 | tf_op jit(solution)/shard_map/all_gather | solution.py:36
  30.4 164.5 %copy-start = (f32[5120]{0:T(1024)S(1)}, f32[5120]{0:T(1024)}, u32[]{:S(2)}) copy-start(f32[5120]{0:T(1024)} %param.8) | copy-start | bytes 61444
Sparse Core Ops, SparseCore 0:
  28.8 102.3 all-reduce.1
Sparse Core Ops, SparseCore 1:
  30.7 62.7 all-gather.4
  94.9 157.4 all-gather.6
  253.8 129.3 all-gather.8
where the time goes:
time: 399 us
  waiting for transfers between devices  276 us (69%)
  blocking collectives  68.4 us (17%)
  matrix products  32.7 us (8%)
  between operations  15.7 us (4%)
    all_gather x1, waiting for transfers between devices, body(): lax.all_gather(w_up, 'col', axis=0, tiled=True)  123 us
    psum x1, waiting for transfers between devices, body(): lax.psum(partial_value, 'row').astype(jnp.float32).astype(jnp.bfloat16)  101 us
    all_to_all x1, blocking collectives, body(): lax.all_to_all(embedded, 'col', split_axis=0, concat_axis=1, tiled=True)  63 us
    all_gather x1, waiting for transfers between devices, body(): lax.all_gather(w_gate, 'col', axis=0, tiled=True)  51 us
    dot_general x3, matrix products, body(): jnp.dot(normed, piece, preferred_element_type=jnp.float32)  20.2 us
    dot_general x1, matrix products, one_block(): jnp.dot(onehot, table_tile, preferred_element_type=jnp.float32)  12.5 us
  transfers between devices with their start and end apart: 4, of which 3 were waited for; matrix products, arithmetic and copies ran while one was open for 4% of the time, Pallas kernels for 0%

commit v1 on v0

v1 whole, which is shorter than its diff:
```python
import functools

import jax
import jax.numpy as jnp
from jax import lax
from jax.experimental import pallas as pl
from jax.experimental.pallas import tpu as pltpu
from jax.sharding import PartitionSpec as P

eps = 1e-05
CHUNKS = 4


def kernel(
    n_row, n_col, chunks, width, features,
    part_ref, gain_ref, wq_hbm, wg_hbm, wu_hbm,
    q_ref, h_ref,
    wq, wg, wu, crs, xsend, xrs, zown, zin, zfar_out, znear_out, act, xbuf, pf, ysend, yrecv,
    w_sem, core_s, core_r, x_s, x_r, zf_s, zn_s, z_r, xa_s, xa_r, ca_s, ca_r, y_s, y_r,
):
    row = lax.axis_index("row")
    col = lax.axis_index("col")
    k = row % 2
    xx = (row // 2) % 2
    z = row // 4
    nz = n_row // 4
    upper = z // (nz // 2)
    sgn = 1 - 2 * upper
    core_peer = row + 1 - 2 * k
    x_peer = row + 2 - 4 * xx
    far_peer = row + 4 * sgn
    near_peer = row - 4 * sgn
    inner = jnp.logical_and(z > 0, z < nz - 1)
    q_own = 2 * k + xx
    q_x = 2 * k + 1 - xx
    q_c0 = 2 * (1 - k) + xx
    q_c1 = 2 * (1 - k) + 1 - xx
    near_slot, far_slot = upper, 1 - upper
    dk = part_ref.shape[3]
    t4 = part_ref.shape[2]
    nq, nf = wq.shape[1], wg.shape[1]
    qo = 2 * nf

    w_copies = [
        pltpu.make_async_copy(wg_hbm, wg, w_sem.at[0]),
        pltpu.make_async_copy(wu_hbm, wu, w_sem.at[1]),
        pltpu.make_async_copy(wq_hbm, wq, w_sem.at[2]),
    ]
    for copy in w_copies:
        copy.start()

    barrier = pltpu.get_barrier_semaphore()

    def greet(where):
        pl.semaphore_signal(barrier, inc=1, device_id=where, device_id_type=pl.DeviceIdType.MESH)

    greet({"row": core_peer})
    greet({"row": x_peer})
    greet({"row": far_peer})
    for d in range(1, n_col):
        greet({"col": (col + d) % n_col})

    @pl.when(inner)
    def _():
        greet({"row": near_peer})

    @pl.when(inner)
    def _():
        pl.semaphore_wait(barrier, 4 + n_col - 1)

    @pl.when(jnp.logical_not(inner))
    def _():
        pl.semaphore_wait(barrier, 3 + n_col - 1)

    def rcopy(src, dst, s, r, where):
        return pltpu.make_async_remote_copy(
            src_ref=src, dst_ref=dst, send_sem=s, recv_sem=r,
            device_id=where, device_id_type=pl.DeviceIdType.MESH,
        )

    def core_rs(c):
        return rcopy(part_ref.at[c, pl.ds(2 * (1 - k), 2)], crs.at[c], core_s.at[c], core_r.at[c], {"row": core_peer})

    def x_rs(c):
        return rcopy(xsend.at[c], xrs.at[c], x_s.at[c], x_r.at[c], {"row": x_peer})

    def z_far_end(c):
        return rcopy(zown.at[c], zin.at[upper, c], zf_s.at[c], z_r.at[upper, c], {"row": far_peer})

    def z_far_inner(c):
        return rcopy(zfar_out.at[c], zin.at[upper, c], zf_s.at[c], z_r.at[upper, c], {"row": far_peer})

    def z_near(c):
        return rcopy(znear_out.at[c], zin.at[1 - upper, c], zn_s.at[c], z_r.at[1 - upper, c], {"row": near_peer})

    def z_wait(slot, c):
        rcopy(zown.at[c], zin.at[slot, c], zf_s.at[c], z_r.at[slot, c], {"row": far_peer}).wait_recv()

    def x_ag(c, q):
        return rcopy(act.at[c, q], act.at[c, q], xa_s.at[c], xa_r.at[c], {"row": x_peer})

    def core_ag(c, q, i):
        return rcopy(act.at[c, q], act.at[c, q], ca_s.at[c, i], ca_r.at[c, i], {"row": core_peer})

    def y_send(c, d):
        peer = (col + d) % n_col
        return rcopy(ysend.at[c, peer], yrecv.at[c, col], y_s.at[c, d - 1], y_r.at[c, col], {"col": peer})

    def y_wait(c, d):
        peer = (col + d) % n_col
        rcopy(ysend.at[c, peer], yrecv.at[c, peer], y_s.at[c, d - 1], y_r.at[c, peer], {"col": peer}).wait_recv()

    def at_stage(t, s, run):
        c = t - s

        @pl.when(jnp.logical_and(c >= 0, c < chunks))
        def _():
            run(c)

    def s0(c):
        core_rs(c).start()

    def s1(c):
        core_rs(c).wait_recv()
        xsend[c] = part_ref[c, q_x] + crs[c, 1 - xx]
        x_rs(c).start()
        zown[c] = part_ref[c, q_own] + crs[c, xx]

    def s2(c):
        x_rs(c).wait_recv()
        zown[c] = zown[c] + xrs[c]

        @pl.when(jnp.logical_not(inner))
        def _():
            z_far_end(c).start()

    def s3(c):
        @pl.when(inner)
        def _():
            z_wait(near_slot, c)
            zfar_out[c] = zown[c] + zin[near_slot, c]
            z_far_inner(c).start()

    def s4(c):
        z_wait(far_slot, c)

        @pl.when(inner)
        def _():
            znear_out[c] = zown[c] + zin[far_slot, c]
            z_near(c).start()
            act[c, q_own] = zfar_out[c] + zin[far_slot, c]

        @pl.when(jnp.logical_not(inner))
        def _():
            act[c, q_own] = zown[c] + zin[far_slot, c]

        x_ag(c, q_own).start()
        core_ag(c, q_own, 0).start()

    def s5(c):
        x_ag(c, q_x).wait_recv()
        core_ag(c, q_x, 1).start()

    def s6(c):
        core_ag(c, q_c0, 0).wait_recv()
        core_ag(c, q_c1, 1).wait_recv()

        @pl.when(c == 0)
        def _():
            for copy in w_copies:
                copy.wait()

        gain = gain_ref[:, pl.ds(pl.multiple_of(col * dk, 128), dk)]
        toks = 4 * t4
        values = act[c].reshape(toks, dk).astype(jnp.float32)
        squares = jnp.sum(values * values, axis=1, keepdims=True)
        xbuf[...] = (values * gain).astype(jnp.bfloat16)
        high = squares.astype(jnp.bfloat16)
        low = (squares - high.astype(jnp.float32)).astype(jnp.bfloat16)
        rows = toks // n_col
        tail = width - qo - nq
        lane = lax.broadcasted_iota(jnp.int32, (toks, tail), 1)
        pf[c, :, :, qo + nq:] = jnp.broadcast_to(squares, (toks, tail)).reshape(n_col, rows, tail)
        both = jnp.where(lane == 0, high.astype(jnp.float32), low.astype(jnp.float32)).astype(jnp.bfloat16)
        ysend[c, :, :, qo + nq:] = both.reshape(n_col, rows, tail)
        tile = 256

        def put(start, out, size):
            out = out.reshape(n_col, rows, size)
            pf[c, :, :, pl.ds(start, size)] = out
            ysend[c, :, :, pl.ds(start, size)] = out.astype(jnp.bfloat16)

        def tiles(j, carry):
            at = pl.multiple_of(j * tile, tile)
            put(at, jnp.dot(xbuf[...], wg[:, pl.ds(at, tile)], preferred_element_type=jnp.float32), tile)
            put(
                pl.multiple_of(nf + j * tile, tile),
                jnp.dot(xbuf[...], wu[:, pl.ds(at, tile)], preferred_element_type=jnp.float32), tile,
            )
            return carry

        lax.fori_loop(0, nf // tile, tiles, 0)
        put(qo, jnp.dot(xbuf[...], wq[...], preferred_element_type=jnp.float32), nq)
        for d in range(1, n_col):
            y_send(c, d).start()

    def s7(c):
        for d in range(1, n_col):
            y_wait(c, d)
        peers = [(col + d) % n_col for d in range(1, n_col)]

        def total(start, size):
            value = pf[c, col, :, start:start + size]
            for peer in peers:
                value = value + yrecv[c, peer, :, start:start + size].astype(jnp.float32)
            return value

        squares = pf[c, col, :, qo + nq:qo + nq + 1]
        for peer in peers:
            squares = squares + yrecv[c, peer, :, qo + nq:qo + nq + 1].astype(jnp.float32)
            squares = squares + yrecv[c, peer, :, qo + nq + 1:qo + nq + 2].astype(jnp.float32)
        factor = lax.rsqrt(squares / features + eps)
        q_ref[c] = (total(qo, nq) * factor).astype(jnp.bfloat16)
        gate = total(0, nf) * factor
        up = total(nf, nf) * factor
        h_ref[c] = (gate / (1.0 + jnp.exp(-gate)) * up).astype(jnp.bfloat16)

    stages = (s0, s1, s2, s3, s4, s5, s6, s7)

    def tick(t, carry):
        for s, run in enumerate(stages):
            at_stage(t, s, run)
        return carry

    lax.fori_loop(0, chunks + len(stages) - 1, tick, 0)

    def finish(c, carry):
        core_rs(c).wait_send()
        x_rs(c).wait_send()
        z_far_end(c).wait_send()

        @pl.when(inner)
        def _():
            z_near(c).wait_send()

        x_ag(c, q_own).wait_send()
        core_ag(c, q_own, 0).wait_send()
        core_ag(c, q_x, 1).wait_send()
        for d in range(1, n_col):
            y_send(c, d).wait_send()
        return carry

    lax.fori_loop(0, chunks, finish, 0)


def body(n_row, n_col, token_ids, table, norm_gain, w_qkv, w_gate, w_up):
    chunks = CHUNKS
    vocab_rows, dk = table.shape
    mine = token_ids.shape[0]
    rows = mine // chunks
    t4 = n_col * rows // 4
    nq, nf = w_qkv.shape[1], w_gate.shape[1]
    width = 2 * nf + (nq + 2 + 127) // 128 * 128
    every_id = lax.all_gather(token_ids, "col", axis=0, tiled=True)
    every_id = every_id.reshape(n_col, chunks, rows).transpose(1, 0, 2).reshape(-1)
    columns = lax.axis_index("row") * vocab_rows + lax.broadcasted_iota(jnp.int32, (1, vocab_rows), 1)
    onehot = (every_id[:, None] == columns).astype(jnp.bfloat16)
    part = jnp.dot(onehot, table, preferred_element_type=jnp.float32).astype(jnp.bfloat16)
    part = part.reshape(chunks, 4, t4, dk)
    bf = jnp.bfloat16
    dma = pltpu.SemaphoreType.DMA
    vmem = pl.BlockSpec(memory_space=pltpu.VMEM)
    hbm = pl.BlockSpec(memory_space=pl.ANY)
    q, h = pl.pallas_call(
        functools.partial(kernel, n_row, n_col, chunks, width, dk * n_col),
        out_shape=(
            jax.ShapeDtypeStruct((chunks, rows, nq), bf),
            jax.ShapeDtypeStruct((chunks, rows, nf), bf),
        ),
        in_specs=[vmem, vmem, hbm, hbm, hbm],
        out_specs=(vmem, vmem),
        scratch_shapes=[
            pltpu.VMEM(w_qkv.shape, bf),
            pltpu.VMEM(w_gate.shape, bf),
            pltpu.VMEM(w_up.shape, bf),
            pltpu.VMEM((chunks, 2, t4, dk), bf),
            pltpu.VMEM((chunks, t4, dk), bf),
            pltpu.VMEM((chunks, t4, dk), bf),
            pltpu.VMEM((chunks, t4, dk), bf),
            pltpu.VMEM((2, chunks, t4, dk), bf),
            pltpu.VMEM((chunks, t4, dk), bf),
            pltpu.VMEM((chunks, t4, dk), bf),
            pltpu.VMEM((chunks, 4, t4, dk), bf),
            pltpu.VMEM((4 * t4, dk), bf),
            pltpu.VMEM((chunks, n_col, rows, width), jnp.float32),
            pltpu.VMEM((chunks, n_col, rows, width), bf),
            pltpu.VMEM((chunks, n_col, rows, width), bf),
            dma((3,)),
            dma((chunks,)), dma((chunks,)),
            dma((chunks,)), dma((chunks,)),
            dma((chunks,)), dma((chunks,)), dma((2, chunks)),
            dma((chunks,)), dma((chunks,)),
            dma((chunks, 2)), dma((chunks, 2)),
            dma((chunks, max(n_col - 1, 1))), dma((chunks, n_col)),
        ],
        compiler_params=pltpu.CompilerParams(
            collective_id=0, has_side_effects=True, vmem_limit_bytes=56 * 1024 * 1024
        ),
    )(part, norm_gain.reshape(1, -1), w_qkv, w_gate, w_up)
    return q.reshape(mine, nq), h.reshape(mine, nf)


def solution(mesh):
    return jax.shard_map(
        functools.partial(body, mesh.shape["row"], mesh.shape["col"]),
        mesh=mesh,
        in_specs=(
            P("col"),
            P("row", "col"),
            P(),
            P("col", "row"),
            P("col", "row"),
            P("col", "row"),
        ),
        out_specs=(P("col", "row"), P("col", "row")),
        check_vma=False,
    )
```

time: 399 us -> 97 us (0.24)
  waiting for transfers between devices: 276 us -> 0 us
  Pallas kernels: 0 us -> 70.4 us
  blocking collectives: 68.4 us -> 5.44 us
  matrix products: 32.7 us -> 13.8 us
  between operations: 15.7 us -> 0.65 us
    all_gather x3 -> x0, waiting for transfers between devices: 174 us -> none  [the longest x1 123 us: body(): lax.all_gather(w_up, 'col', axis=0, tiled=True)]
    psum x1 -> x0, waiting for transfers between devices: 101 us -> none  [body(): lax.psum(partial_value, 'row').astype(jnp.float32).astype(jnp.bfloat16)]
    pallas_call x0 -> x1, Pallas kernels: none -> 70.4 us  [body(): pl.pallas_call(functools.partial(kernel, n_row, n_col, chunks, width, dk...]
    all_to_all x1 -> x0, blocking collectives: 63 us -> none  [body(): lax.all_to_all(embedded, 'col', split_axis=0, concat_axis=1, tiled=True)]
    dot_general x4 -> x1, matrix products: 32.7 us -> 13.8 us  [body(): jnp.dot(onehot, table, preferred_element_type=jnp.float32)]
    unnamed x2 -> x5, local copies, waits for them, and re-layouts: 0.01 us -> 6.25 us
  transfers between devices with their start and end apart: 4 -> 0, of which waited for: 3 -> 0; matrix products, arithmetic and copies ran while one was open for 4% -> 0% of each run, Pallas kernels for 0% -> 0%
where the time goes in v1:
time: 97 us; the launch traced here: 96.8 us
  Pallas kernels  70.4 us (73%)
  matrix products  13.8 us (14%)
  local copies, waits for them, and re-layouts  6.43 us (7%)
  blocking collectives  5.44 us (6%)
    pallas_call x1, Pallas kernels, body(): pl.pallas_call(functools.partial(kernel, n_row, n_col, chunks, width, dk...  70.4 us
    dot_general x1, matrix products, body(): jnp.dot(onehot, table, preferred_element_type=jnp.float32)  13.8 us
    unnamed x5, local copies, waits for them, and re-layouts  6.25 us
    all_gather x1, blocking collectives, body(): every_id = lax.all_gather(token_ids, 'col', axis=0, tiled=True)  5.44 us

profile of v1, /device:TPU:0, one launch (start us, length us, event | category | flops | bytes accessed | tf_op | source)
XLA Modules:
  0.0 96.8 jit_solution(16142975096576308136)
XLA Ops:
  0.6 5.4 %all-gather = s32[2,1,256]{2,1,0:T(1,128)S(1)} all-gather(s32[1,1,256]{2,1,0:T(1,128)} %bitcast.12), channel_id=1, replica_groups=mesh['row'=16,'col'=2] {'col'}, dimensions={0}, use_global_device_ids=true | all-gather | bytes 3072 | tf_op jit(solution)/shard_map/all_gather | solution.py:264
  6.1 0.1 reshape.25
  6.2 0.1 eq.15
  6.3 0.0 copy-start
  6.3 13.8 %fusion.2 = bf16[512,2560]{1,0:T(8,128)(2,1)} fusion(bf16[3160,2560]{1,0:T(8,128)(2,1)} %param.7, s32[3160]{0:T(1024)S(1)} %iota_add_fusion, s32[512]{0:T(512)S(1)} %eq.15), kind=kOutput, calls=%fused_computation.2 | convolution fusion | flops 8286679040 | bytes 18815328 | tf_op jit(solution)/shard_map/dot_general | solution.py:268
  20.1 0.0 copy-done
  20.1 2.6 %copy.16.wq_hbm = bf16[2560,448]{1,0:T(8,128)(2,1)} copy(bf16[2560,448]{0,1:T(8,128)(2,1)S(1)} %copy-done) | data formatting | bytes 4587520 | tf_op args[3]
  22.7 70.4 %shard_map.77 = (bf16[4,64,448]{2,1,0:T(8,128)(2,1)}, bf16[4,64,1024]{2,1,0:T(8,128)(2,1)}) custom-call(bf16[4,4,32,2560]{3,2,1,0:T(8,128)(2,1)} %bitcast.7, f32[1,5120]{1,0:T(1,128)} %bitcast.10, bf16[2560,448]{1,0:T(8,128)(2,1)} %copy.16.wq_hbm, bf16[2560,1024]{1,0:T(8,128)(2,1)} %wg_hbm.1, bf16[2560,1024]{1,0:T(8,128)(2,1)} %wu_hbm.1), custom_call_target="tpu_custom_call" | custom-call | tf_op jit(solution)/shard_map/pallas_call | solution.py:274
  93.1 1.8 %copy.17 = bf16[256,448]{0,1:T(8,128)(2,1)} copy(bf16[256,448]{1,0:T(8,128)(2,1)} %bitcast.9) | data formatting | bytes 458752
  94.9 1.9 %copy.19 = bf16[256,1024]{1,0:T(8,128)(2,1)} copy(bf16[256,1024]{1,0:T(8,128)(2,1)} %bitcast.8) | data formatting | bytes 1048576
  (3 shorter events, 0.0 us)
Async XLA Ops:
  6.3 13.8 %copy-start = (bf16[2560,448]{0,1:T(8,128)(2,1)S(1)}, bf16[2560,448]{0,1:T(8,128)(2,1)}, u32[]{:S(2)}) copy-start(bf16[2560,448]{0,1:T(8,128)(2,1)} %param.9) | copy-start | bytes 6881284

commit v2 on v1

--- a/solution.py
+++ b/solution.py
@@ -9,14 +9,15 @@
 
 eps = 1e-05
 CHUNKS = 4
+TILE = 256
 
 
 def kernel(
     n_row, n_col, chunks, width, features,
-    part_ref, gain_ref, wq_hbm, wg_hbm, wu_hbm,
+    ids_ref, table_hbm, gain_ref, wq_hbm, wg_hbm, wu_hbm,
     q_ref, h_ref,
-    wq, wg, wu, crs, xsend, xrs, zown, zin, zfar_out, znear_out, act, xbuf, pf, ysend, yrecv,
-    w_sem, core_s, core_r, x_s, x_r, zf_s, zn_s, z_r, xa_s, xa_r, ca_s, ca_r, y_s, y_r,
+    tab, idbuf, onehot, part_ref, wq, wg, wu, crs, xsend, xrs, zown, zin, zfar_out, znear_out, act, xbuf, pf, ysend, yrecv,
+    t_sem, id_s, id_r, w_sem, core_s, core_r, x_s, x_r, zf_s, zn_s, z_r, xa_s, xa_r, ca_s, ca_r, y_s, y_r,
 ):
     row = lax.axis_index("row")
     col = lax.axis_index("col")
@@ -38,16 +39,31 @@
     near_slot, far_slot = upper, 1 - upper
     dk = part_ref.shape[3]
     t4 = part_ref.shape[2]
-    nq, nf = wq.shape[1], wg.shape[1]
+    nq, nf = wq.shape[0], wg.shape[1]
     qo = 2 * nf
+    pieces = nf // TILE
+    vocab = table_hbm.shape[0]
+    n_tab, vocab_pad, tab_tile = tab.shape
+    rows = ids_ref.shape[1]
+    toks = n_col * rows
 
     w_copies = [
         pltpu.make_async_copy(wg_hbm, wg, w_sem.at[0]),
         pltpu.make_async_copy(wu_hbm, wu, w_sem.at[1]),
         pltpu.make_async_copy(wq_hbm, wq, w_sem.at[2]),
     ]
-    for copy in w_copies:
-        copy.start()
+
+    def table_copy(i):
+        return pltpu.make_async_copy(
+            table_hbm.at[:, pl.ds(pl.multiple_of(i * tab_tile, 128), tab_tile)],
+            tab.at[i, pl.ds(0, vocab)], t_sem.at[i],
+        )
+
+    clear = vocab // 16 * 16
+    if vocab_pad > clear:
+        tab[:, clear:, :] = jnp.zeros((n_tab, vocab_pad - clear, tab_tile), tab.dtype)
+    for i in range(n_tab):
+        table_copy(i).start()
 
     barrier = pltpu.get_barrier_semaphore()
 
@@ -102,13 +118,36 @@
     def core_ag(c, q, i):
         return rcopy(act.at[c, q], act.at[c, q], ca_s.at[c, i], ca_r.at[c, i], {"row": core_peer})
 
-    def y_send(c, d):
+    def id_send(d):
         peer = (col + d) % n_col
-        return rcopy(ysend.at[c, peer], yrecv.at[c, col], y_s.at[c, d - 1], y_r.at[c, col], {"col": peer})
-
-    def y_wait(c, d):
+        return rcopy(ids_ref, idbuf.at[col], id_s.at[d - 1], id_r.at[col], {"col": peer})
+
+    def id_wait(d):
         peer = (col + d) % n_col
-        rcopy(ysend.at[c, peer], yrecv.at[c, peer], y_s.at[c, d - 1], y_r.at[c, peer], {"col": peer}).wait_recv()
+        rcopy(ids_ref, idbuf.at[peer], id_s.at[d - 1], id_r.at[peer], {"col": peer}).wait_recv()
+
+    for d in range(1, n_col):
+        id_send(d).start()
+
+    def y_lanes(j):
+        if isinstance(j, int) and j == pieces:
+            return pl.ds(qo, width - qo)
+        return pl.ds(pl.multiple_of(j * 2 * TILE, 128), 2 * TILE)
+
+    def y_copy(c, d, j, slot):
+        peer = (col + d) % n_col
+        at = y_lanes(j)
+        return rcopy(
+            ysend.at[c, peer, :, at], yrecv.at[c, slot, :, at],
+            y_s.at[c, d - 1, j], y_r.at[c, slot, j], {"col": peer},
+        )
+
+    def y_send(c, d, j):
+        return y_copy(c, d, j, col)
+
+    def y_wait(c, j):
+        for d in range(1, n_col):
+            y_copy(c, d, j, (col + d) % n_col).wait_recv()
 
     def at_stage(t, s, run):
         c = t - s
@@ -118,7 +157,37 @@
             run(c)
 
     def s0(c):
+        @pl.when(c == 0)
+        def _():
+            for d in range(1, n_col):
+                id_wait(d)
+
+        base = row * vocab
+        lane = lax.broadcasted_iota(jnp.int32, (rows, 128), 1)
+        for d in range(n_col):
+            at = (col + d) % n_col
+            local = (ids_ref[c] if d == 0 else idbuf[at, c]) - base - lane
+            for i in range(vocab_pad // 128):
+                hit = jnp.where(local == i * 128, 1.0, 0.0).astype(jnp.bfloat16)
+                onehot[at, :, i * 128:(i + 1) * 128] = hit
+
+        def columns(i, carry):
+            @pl.when(c == 0)
+            def _():
+                table_copy(i).wait()
+
+            found = jnp.dot(onehot[...].reshape(toks, vocab_pad), tab[i], preferred_element_type=jnp.float32)
+            at = pl.ds(pl.multiple_of(i * tab_tile, 128), tab_tile)
+            part_ref[c, :, :, at] = found.astype(jnp.bfloat16).reshape(4, t4, tab_tile)
+            return carry
+
+        lax.fori_loop(0, n_tab, columns, 0)
         core_rs(c).start()
+
+        @pl.when(c == 0)
+        def _():
+            for copy in w_copies:
+                copy.start()
 
     def s1(c):
         core_rs(c).wait_recv()
@@ -171,64 +240,76 @@
                 copy.wait()
 
         gain = gain_ref[:, pl.ds(pl.multiple_of(col * dk, 128), dk)]
-        toks = 4 * t4
         values = act[c].reshape(toks, dk).astype(jnp.float32)
         squares = jnp.sum(values * values, axis=1, keepdims=True)
         xbuf[...] = (values * gain).astype(jnp.bfloat16)
         high = squares.astype(jnp.bfloat16)
         low = (squares - high.astype(jnp.float32)).astype(jnp.bfloat16)
-        rows = toks // n_col
         tail = width - qo - nq
         lane = lax.broadcasted_iota(jnp.int32, (toks, tail), 1)
         pf[c, :, :, qo + nq:] = jnp.broadcast_to(squares, (toks, tail)).reshape(n_col, rows, tail)
         both = jnp.where(lane == 0, high.astype(jnp.float32), low.astype(jnp.float32)).astype(jnp.bfloat16)
         ysend[c, :, :, qo + nq:] = both.reshape(n_col, rows, tail)
-        tile = 256
 
         def put(start, out, size):
             out = out.reshape(n_col, rows, size)
             pf[c, :, :, pl.ds(start, size)] = out
             ysend[c, :, :, pl.ds(start, size)] = out.astype(jnp.bfloat16)
 
+        put(
+            qo,
+            lax.dot_general(xbuf[...], wq[...], (((1,), (1,)), ((), ())), preferred_element_type=jnp.float32), nq,
+        )
+        for d in range(1, n_col):
+            y_send(c, d, pieces).start()
+
         def tiles(j, carry):
-            at = pl.multiple_of(j * tile, tile)
-            put(at, jnp.dot(xbuf[...], wg[:, pl.ds(at, tile)], preferred_element_type=jnp.float32), tile)
+            at = pl.ds(pl.multiple_of(j * TILE, TILE), TILE)
+            start = pl.multiple_of(2 * j * TILE, TILE)
+            put(start, jnp.dot(xbuf[...], wg[:, at], preferred_element_type=jnp.float32), TILE)
             put(
-                pl.multiple_of(nf + j * tile, tile),
-                jnp.dot(xbuf[...], wu[:, pl.ds(at, tile)], preferred_element_type=jnp.float32), tile,
+                pl.multiple_of(start + TILE, TILE),
+                jnp.dot(xbuf[...], wu[:, at], preferred_element_type=jnp.float32), TILE,
             )
+            for d in range(1, n_col):
+                y_send(c, d, j).start()
             return carry
 
-        lax.fori_loop(0, nf // tile, tiles, 0)
-        put(qo, jnp.dot(xbuf[...], wq[...], preferred_element_type=jnp.float32), nq)
-        for d in range(1, n_col):
-            y_send(c, d).start()
+        lax.fori_loop(0, pieces, tiles, 0)
 
     def s7(c):
-        for d in range(1, n_col):
-            y_wait(c, d)
         peers = [(col + d) % n_col for d in range(1, n_col)]
 
         def total(start, size):
-            value = pf[c, col, :, start:start + size]
+            at = pl.ds(start, size)
+            value = pf[c, col, :, at]
             for peer in peers:
-                value = value + yrecv[c, peer, :, start:start + size].astype(jnp.float32)
+                value = value + yrecv[c, peer, :, at].astype(jnp.float32)
             return value
 
+        y_wait(c, pieces)
         squares = pf[c, col, :, qo + nq:qo + nq + 1]
         for peer in peers:
             squares = squares + yrecv[c, peer, :, qo + nq:qo + nq + 1].astype(jnp.float32)
             squares = squares + yrecv[c, peer, :, qo + nq + 1:qo + nq + 2].astype(jnp.float32)
         factor = lax.rsqrt(squares / features + eps)
         q_ref[c] = (total(qo, nq) * factor).astype(jnp.bfloat16)
-        gate = total(0, nf) * factor
-        up = total(nf, nf) * factor
-        h_ref[c] = (gate / (1.0 + jnp.exp(-gate)) * up).astype(jnp.bfloat16)
-
-    stages = (s0, s1, s2, s3, s4, s5, s6, s7)
+
+        def tiles(j, carry):
+            y_wait(c, j)
+            start = pl.multiple_of(2 * j * TILE, TILE)
+            gate = total(start, TILE) * factor
+            up = total(pl.multiple_of(start + TILE, TILE), TILE) * factor
+            at = pl.ds(pl.multiple_of(j * TILE, TILE), TILE)
+            h_ref[c, :, at] = (gate / (1.0 + jnp.exp(-gate)) * up).astype(jnp.bfloat16)
+            return carry
+
+        lax.fori_loop(0, pieces, tiles, 0)
+
+    stages = ((1, s1), (2, s2), (3, s3), (4, s4), (5, s5), (0, s0), (6, s6), (7, s7))
 
     def tick(t, carry):
-        for s, run in enumerate(stages):
+        for s, run in stages:
             at_stage(t, s, run)
         return carry
 
@@ -247,10 +328,13 @@
         core_ag(c, q_own, 0).wait_send()
         core_ag(c, q_x, 1).wait_send()
         for d in range(1, n_col):
-            y_send(c, d).wait_send()
+            for j in range(pieces + 1):
+                y_send(c, d, j).wait_send()
         return carry
 
     lax.fori_loop(0, chunks, finish, 0)
+    for d in range(1, n_col):
+        id_send(d).wait_send()
 
 
 def body(n_row, n_col, token_ids, table, norm_gain, w_qkv, w_gate, w_up):
@@ -261,12 +345,11 @@
     t4 = n_col * rows // 4
     nq, nf = w_qkv.shape[1], w_gate.shape[1]
     width = 2 * nf + (nq + 2 + 127) // 128 * 128
-    every_id = lax.all_gather(token_ids, "col", axis=0, tiled=True)
-    every_id = every_id.reshape(n_col, chunks, rows).transpose(1, 0, 2).reshape(-1)
-    columns = lax.axis_index("row") * vocab_rows + lax.broadcasted_iota(jnp.int32, (1, vocab_rows), 1)
-    onehot = (every_id[:, None] == columns).astype(jnp.bfloat16)
-    part = jnp.dot(onehot, table, preferred_element_type=jnp.float32).astype(jnp.bfloat16)
-    part = part.reshape(chunks, 4, t4, dk)
+    ids = jnp.broadcast_to(token_ids.reshape(chunks, rows, 1), (chunks, rows, 128))
+    tab_tile = 512 if dk % 512 == 0 else 128
+    n_tab = dk // tab_tile
+    vocab_pad = (vocab_rows + 127) // 128 * 128
+    pieces = nf // TILE
     bf = jnp.bfloat16
     dma = pltpu.SemaphoreType.DMA
     vmem = pl.BlockSpec(memory_space=pltpu.VMEM)
@@ -277,10 +360,14 @@
             jax.ShapeDtypeStruct((chunks, rows, nq), bf),
             jax.ShapeDtypeStruct((chunks, rows, nf), bf),
         ),
-        in_specs=[vmem, vmem, hbm, hbm, hbm],
+        in_specs=[vmem, hbm, vmem, hbm, hbm, hbm],
         out_specs=(vmem, vmem),
         scratch_shapes=[
-            pltpu.VMEM(w_qkv.shape, bf),
+            pltpu.VMEM((n_tab, vocab_pad, tab_tile), bf),
+            pltpu.VMEM((n_col, chunks, rows, 128), jnp.int32),
+            pltpu.VMEM((n_col, rows, vocab_pad), bf),
+            pltpu.VMEM((chunks, 4, t4, dk), bf),
+            pltpu.VMEM((nq, dk), bf),
             pltpu.VMEM(w_gate.shape, bf),
             pltpu.VMEM(w_up.shape, bf),
             pltpu.VMEM((chunks, 2, t4, dk), bf),
@@ -295,18 +382,19 @@
             pltpu.VMEM((chunks, n_col, rows, width), jnp.float32),
             pltpu.VMEM((chunks, n_col, rows, width), bf),
             pltpu.VMEM((chunks, n_col, rows, width), bf),
+            dma((n_tab,)), dma((max(n_col - 1, 1),)), dma((n_col,)),
             dma((3,)),
             dma((chunks,)), dma((chunks,)),
             dma((chunks,)), dma((chunks,)),
             dma((chunks,)), dma((chunks,)), dma((2, chunks)),
             dma((chunks,)), dma((chunks,)),
             dma((chunks, 2)), dma((chunks, 2)),
-            dma((chunks, max(n_col - 1, 1))), dma((chunks, n_col)),
+            dma((chunks, max(n_col - 1, 1), pieces + 1)), dma((chunks, n_col, pieces + 1)),
         ],
         compiler_params=pltpu.CompilerParams(
-            collective_id=0, has_side_effects=True, vmem_limit_bytes=56 * 1024 * 1024
+            collective_id=0, has_side_effects=True, vmem_limit_bytes=62 * 1024 * 1024
         ),
-    )(part, norm_gain.reshape(1, -1), w_qkv, w_gate, w_up)
+    )(ids, table, norm_gain.reshape(1, -1), w_qkv.T, w_gate, w_up)
     return q.reshape(mine, nq), h.reshape(mine, nf)
 
 

time: 97 us -> 83.3 us (0.86)
  matrix products: 13.8 us -> 0 us
  Pallas kernels: 70.4 us -> 77.3 us
  blocking collectives: 5.44 us -> 0 us
  local copies, waits for them, and re-layouts: 6.43 us -> 5.16 us
    dot_general x1 -> x0, matrix products: 13.8 us -> none  [body(): jnp.dot(onehot, table, preferred_element_type=jnp.float32)]
    pallas_call x1, Pallas kernels: 70.4 us -> 77.3 us  [body(): pl.pallas_call(functools.partial(kernel, n_row, n_col, chunks, width, dk...]
    all_gather x1 -> x0, blocking collectives: 5.44 us -> none  [body(): every_id = lax.all_gather(token_ids, 'col', axis=0, tiled=True)]
    unnamed x5 -> x2, local copies, waits for them, and re-layouts: 6.25 us -> 3.64 us
    broadcast_in_dim x0 -> x2, local copies, waits for them, and re-layouts: none -> 1.52 us  [body(): jnp.broadcast_to(token_ids.reshape(chunks, rows, 1), (chunks, rows, 128))]
where the time goes in v2:
time: 83.3 us; the launch traced here: 83.1 us
  Pallas kernels  77.3 us (93%)
  local copies, waits for them, and re-layouts  5.16 us (6%)
    pallas_call x1, Pallas kernels, body(): pl.pallas_call(functools.partial(kernel, n_row, n_col, chunks, width, dk...  77.3 us
    unnamed x2, local copies, waits for them, and re-layouts  3.64 us

profile of v2, /device:TPU:0, one launch (start us, length us, event | category | flops | bytes accessed | tf_op | source)
XLA Modules:
  0.0 83.1 jit_solution(10679066773945258762)
XLA Ops:
  0.6 0.8 broadcast_in_dim.7
  1.4 0.8 broadcast_in_dim.8.ids_ref
  2.1 77.3 %shard_map.77 = (bf16[4,64,448]{2,1,0:T(8,128)(2,1)}, bf16[4,64,1024]{2,1,0:T(8,128)(2,1)}) custom-call(s32[4,64,128]{2,1,0:T(8,128)} %broadcast_in_dim.8.ids_ref, bf16[3160,2560]{1,0:T(8,128)(2,1)} %table_hbm.1, f32[1,5120]{1,0:T(1,128)} %bitcast.7, bf16[448,2560]{1,0:T(8,128)(2,1)} %bitcast.4, bf16[2560,1024]{1,0:T(8,128)(2,1)} %wg_hbm.1, ...), custom_call_target="tpu_custom_call" | custom-call | tf_op jit(solution)/shard_map/pallas_call | solution.py:357
  79.4 1.8 %copy.8 = bf16[256,448]{0,1:T(8,128)(2,1)} copy(bf16[256,448]{1,0:T(8,128)(2,1)} %bitcast.6) | data formatting | bytes 458752
  81.2 1.9 %copy.10 = bf16[256,1024]{1,0:T(8,128)(2,1)} copy(bf16[256,1024]{1,0:T(8,128)(2,1)} %bitcast.5) | data formatting | bytes 1048576

commit v3 on v2

--- a/solution.py
+++ b/solution.py
@@ -8,12 +8,12 @@
 from jax.sharding import PartitionSpec as P
 
 eps = 1e-05
-CHUNKS = 4
+BLOCKS = 4
 TILE = 256
 
 
 def kernel(
-    n_row, n_col, chunks, width, features,
+    n_row, n_col, blocks, width, features,
     ids_ref, table_hbm, gain_ref, wq_hbm, wg_hbm, wu_hbm,
     q_ref, h_ref,
     tab, idbuf, onehot, part_ref, wq, wg, wu, crs, xsend, xrs, zown, zin, zfar_out, znear_out, act, xbuf, pf, ysend, yrecv,
@@ -46,6 +46,8 @@
     n_tab, vocab_pad, tab_tile = tab.shape
     rows = ids_ref.shape[1]
     toks = n_col * rows
+    chunks = 2 * blocks
+    half_tab, half_pieces = n_tab // 2, pieces // 2
 
     w_copies = [
         pltpu.make_async_copy(wg_hbm, wg, w_sem.at[0]),
@@ -156,35 +158,48 @@
         def _():
             run(c)
 
-    def s0(c):
-        @pl.when(c == 0)
-        def _():
-            for d in range(1, n_col):
-                id_wait(d)
-
+    def fill_onehot(b):
         base = row * vocab
         lane = lax.broadcasted_iota(jnp.int32, (rows, 128), 1)
         for d in range(n_col):
             at = (col + d) % n_col
-            local = (ids_ref[c] if d == 0 else idbuf[at, c]) - base - lane
+            local = (ids_ref[b] if d == 0 else idbuf[at, b]) - base - lane
             for i in range(vocab_pad // 128):
                 hit = jnp.where(local == i * 128, 1.0, 0.0).astype(jnp.bfloat16)
                 onehot[at, :, i * 128:(i + 1) * 128] = hit
 
+    def lookup(t):
+        odd = t % 2
+        b = (t + 1) // 2
+
+        @pl.when(t == 0)
+        def _():
+            for d in range(1, n_col):
+                id_wait(d)
+
+        @pl.when(jnp.logical_or(t == 0, odd == 1))
+        def _():
+            fill_onehot(b)
+
         def columns(i, carry):
-            @pl.when(c == 0)
+            @pl.when(t == 0)
             def _():
                 table_copy(i).wait()
 
             found = jnp.dot(onehot[...].reshape(toks, vocab_pad), tab[i], preferred_element_type=jnp.float32)
             at = pl.ds(pl.multiple_of(i * tab_tile, 128), tab_tile)
-            part_ref[c, :, :, at] = found.astype(jnp.bfloat16).reshape(4, t4, tab_tile)
+            part_ref[pl.ds(2 * b, 2), :, :, at] = found.astype(jnp.bfloat16).reshape(2, 4, t4, tab_tile)
             return carry
 
-        lax.fori_loop(0, n_tab, columns, 0)
-        core_rs(c).start()
-
-        @pl.when(c == 0)
+        first = (1 - odd) * jnp.minimum(t, 1) * half_tab
+        lax.fori_loop(first, odd * half_tab + (1 - odd) * n_tab, columns, 0)
+
+        @pl.when(odd == 0)
+        def _():
+            core_rs(t).start()
+            core_rs(t + 1).start()
+
+        @pl.when(t == 0)
         def _():
             for copy in w_copies:
                 copy.start()
@@ -230,9 +245,15 @@
         x_ag(c, q_x).wait_recv()
         core_ag(c, q_x, 1).start()
 
-    def s6(c):
-        core_ag(c, q_c0, 0).wait_recv()
-        core_ag(c, q_c1, 1).wait_recv()
+    def put(c, start, out, size):
+        out = out.reshape(n_col, rows, size)
+        pf[c, :, :, pl.ds(start, size)] = out
+        ysend[c, :, :, pl.ds(start, size)] = out.astype(jnp.bfloat16)
+
+    def prepare(c):
+        for i in range(2):
+            core_ag(2 * c + i, q_c0, 0).wait_recv()
+            core_ag(2 * c + i, q_c1, 1).wait_recv()
 
         @pl.when(c == 0)
         def _():
@@ -240,7 +261,7 @@
                 copy.wait()
 
         gain = gain_ref[:, pl.ds(pl.multiple_of(col * dk, 128), dk)]
-        values = act[c].reshape(toks, dk).astype(jnp.float32)
+        values = act[pl.ds(2 * c, 2)].reshape(toks, dk).astype(jnp.float32)
         squares = jnp.sum(values * values, axis=1, keepdims=True)
         xbuf[...] = (values * gain).astype(jnp.bfloat16)
         high = squares.astype(jnp.bfloat16)
@@ -251,31 +272,27 @@
         both = jnp.where(lane == 0, high.astype(jnp.float32), low.astype(jnp.float32)).astype(jnp.bfloat16)
         ysend[c, :, :, qo + nq:] = both.reshape(n_col, rows, tail)
 
-        def put(start, out, size):
-            out = out.reshape(n_col, rows, size)
-            pf[c, :, :, pl.ds(start, size)] = out
-            ysend[c, :, :, pl.ds(start, size)] = out.astype(jnp.bfloat16)
-
         put(
-            qo,
+            c, qo,
             lax.dot_general(xbuf[...], wq[...], (((1,), (1,)), ((), ())), preferred_element_type=jnp.float32), nq,
         )
         for d in range(1, n_col):
             y_send(c, d, pieces).start()
 
+    def products(c, first, last):
         def tiles(j, carry):
             at = pl.ds(pl.multiple_of(j * TILE, TILE), TILE)
             start = pl.multiple_of(2 * j * TILE, TILE)
-            put(start, jnp.dot(xbuf[...], wg[:, at], preferred_element_type=jnp.float32), TILE)
+            put(c, start, jnp.dot(xbuf[...], wg[:, at], preferred_element_type=jnp.float32), TILE)
             put(
-                pl.multiple_of(start + TILE, TILE),
+                c, pl.multiple_of(start + TILE, TILE),
                 jnp.dot(xbuf[...], wu[:, at], preferred_element_type=jnp.float32), TILE,
             )
             for d in range(1, n_col):
                 y_send(c, d, j).start()
             return carry
 
-        lax.fori_loop(0, pieces, tiles, 0)
+        lax.fori_loop(first, last, tiles, 0)
 
     def s7(c):
         peers = [(col + d) % n_col for d in range(1, n_col)]
@@ -306,14 +323,35 @@
 
         lax.fori_loop(0, pieces, tiles, 0)
 
-    stages = ((1, s1), (2, s2), (3, s3), (4, s4), (5, s5), (0, s0), (6, s6), (7, s7))
+    stages = ((1, s1), (2, s2), (3, s3), (4, s4), (5, s5))
 
     def tick(t, carry):
         for s, run in stages:
             at_stage(t, s, run)
+
+        @pl.when(t < chunks - 1)
+        def _():
+            lookup(t)
+
+        since = t - 7
+        b = (t - 7) // 2
+
+        @pl.when(jnp.logical_and(since >= 0, since < chunks))
+        def _():
+            odd = since % 2
+
+            @pl.when(odd == 0)
+            def _():
+                prepare(b)
+
+            products(b, odd * half_pieces, (1 - odd) * half_pieces + odd * pieces)
+
+            @pl.when(odd == 1)
+            def _():
+                s7(b)
         return carry
 
-    lax.fori_loop(0, chunks + len(stages) - 1, tick, 0)
+    lax.fori_loop(0, chunks + 7, tick, 0)
 
     def finish(c, carry):
         core_rs(c).wait_send()
@@ -327,26 +365,31 @@
         x_ag(c, q_own).wait_send()
         core_ag(c, q_own, 0).wait_send()
         core_ag(c, q_x, 1).wait_send()
+        return carry
+
+    def finish_y(c, carry):
         for d in range(1, n_col):
             for j in range(pieces + 1):
                 y_send(c, d, j).wait_send()
         return carry
 
     lax.fori_loop(0, chunks, finish, 0)
+    lax.fori_loop(0, blocks, finish_y, 0)
     for d in range(1, n_col):
         id_send(d).wait_send()
 
 
 def body(n_row, n_col, token_ids, table, norm_gain, w_qkv, w_gate, w_up):
-    chunks = CHUNKS
+    blocks = BLOCKS
+    chunks = 2 * blocks
     vocab_rows, dk = table.shape
     mine = token_ids.shape[0]
-    rows = mine // chunks
-    t4 = n_col * rows // 4
+    rows = mine // blocks
+    t4 = n_col * rows // 8
     nq, nf = w_qkv.shape[1], w_gate.shape[1]
     width = 2 * nf + (nq + 2 + 127) // 128 * 128
-    ids = jnp.broadcast_to(token_ids.reshape(chunks, rows, 1), (chunks, rows, 128))
-    tab_tile = 512 if dk % 512 == 0 else 128
+    ids = jnp.broadcast_to(token_ids.reshape(blocks, rows, 1), (blocks, rows, 128))
+    tab_tile = 256 if dk % 256 == 0 else 128
     n_tab = dk // tab_tile
     vocab_pad = (vocab_rows + 127) // 128 * 128
     pieces = nf // TILE
@@ -355,16 +398,16 @@
     vmem = pl.BlockSpec(memory_space=pltpu.VMEM)
     hbm = pl.BlockSpec(memory_space=pl.ANY)
     q, h = pl.pallas_call(
-        functools.partial(kernel, n_row, n_col, chunks, width, dk * n_col),
+        functools.partial(kernel, n_row, n_col, blocks, width, dk * n_col),
         out_shape=(
-            jax.ShapeDtypeStruct((chunks, rows, nq), bf),
-            jax.ShapeDtypeStruct((chunks, rows, nf), bf),
+            jax.ShapeDtypeStruct((blocks, rows, nq), bf),
+            jax.ShapeDtypeStruct((blocks, rows, nf), bf),
         ),
         in_specs=[vmem, hbm, vmem, hbm, hbm, hbm],
         out_specs=(vmem, vmem),
         scratch_shapes=[
             pltpu.VMEM((n_tab, vocab_pad, tab_tile), bf),
-            pltpu.VMEM((n_col, chunks, rows, 128), jnp.int32),
+            pltpu.VMEM((n_col, blocks, rows, 128), jnp.int32),
             pltpu.VMEM((n_col, rows, vocab_pad), bf),
             pltpu.VMEM((chunks, 4, t4, dk), bf),
             pltpu.VMEM((nq, dk), bf),
@@ -378,10 +421,10 @@
             pltpu.VMEM((chunks, t4, dk), bf),
             pltpu.VMEM((chunks, t4, dk), bf),
             pltpu.VMEM((chunks, 4, t4, dk), bf),
-            pltpu.VMEM((4 * t4, dk), bf),
-            pltpu.VMEM((chunks, n_col, rows, width), jnp.float32),
-            pltpu.VMEM((chunks, n_col, rows, width), bf),
-            pltpu.VMEM((chunks, n_col, rows, width), bf),
+            pltpu.VMEM((n_col * rows, dk), bf),
+            pltpu.VMEM((blocks, n_col, rows, width), jnp.float32),
+            pltpu.VMEM((blocks, n_col, rows, width), bf),
+            pltpu.VMEM((blocks, n_col, rows, width), bf),
             dma((n_tab,)), dma((max(n_col - 1, 1),)), dma((n_col,)),
             dma((3,)),
             dma((chunks,)), dma((chunks,)),
@@ -389,7 +432,7 @@
             dma((chunks,)), dma((chunks,)), dma((2, chunks)),
             dma((chunks,)), dma((chunks,)),
             dma((chunks, 2)), dma((chunks, 2)),
-            dma((chunks, max(n_col - 1, 1), pieces + 1)), dma((chunks, n_col, pieces + 1)),
+            dma((blocks, max(n_col - 1, 1), pieces + 1)), dma((blocks, n_col, pieces + 1)),
         ],
         compiler_params=pltpu.CompilerParams(
             collective_id=0, has_side_effects=True, vmem_limit_bytes=62 * 1024 * 1024

time: 83.3 us -> 91.3 us (1.096)
  Pallas kernels: 77.3 us -> 85.3 us
    pallas_call x1, Pallas kernels: 77.3 us -> 85.3 us  [body(): pl.pallas_call(functools.partial(kernel, n_row, n_col, blocks, width, dk...]
where the time goes in v3:
time: 91.3 us; the launch traced here: 91.1 us
  Pallas kernels  85.3 us (93%)
  local copies, waits for them, and re-layouts  5.16 us (6%)
    pallas_call x1, Pallas kernels, body(): pl.pallas_call(functools.partial(kernel, n_row, n_col, blocks, width, dk...  85.3 us
    unnamed x2, local copies, waits for them, and re-layouts  3.64 us

profile of v3, /device:TPU:0, one launch (start us, length us, event | category | flops | bytes accessed | tf_op | source)
XLA Modules:
  0.0 91.1 jit_solution(17455780412714125387)
XLA Ops:
  0.6 0.8 broadcast_in_dim.7
  1.4 0.8 broadcast_in_dim.8.ids_ref
  2.1 85.3 %shard_map.77 = (bf16[4,64,448]{2,1,0:T(8,128)(2,1)}, bf16[4,64,1024]{2,1,0:T(8,128)(2,1)}) custom-call(s32[4,64,128]{2,1,0:T(8,128)} %broadcast_in_dim.8.ids_ref, bf16[3160,2560]{1,0:T(8,128)(2,1)} %table_hbm.1, f32[1,5120]{1,0:T(1,128)} %bitcast.7, bf16[448,2560]{1,0:T(8,128)(2,1)} %bitcast.4, bf16[2560,1024]{1,0:T(8,128)(2,1)} %wg_hbm.1, ...), custom_call_target="tpu_custom_call" | custom-call | tf_op jit(solution)/shard_map/pallas_call | solution.py:400
  87.4 1.8 %copy.8 = bf16[256,448]{0,1:T(8,128)(2,1)} copy(bf16[256,448]{1,0:T(8,128)(2,1)} %bitcast.6) | data formatting | bytes 458752
  89.2 1.9 %copy.10 = bf16[256,1024]{1,0:T(8,128)(2,1)} copy(bf16[256,1024]{1,0:T(8,128)(2,1)} %bitcast.5) | data formatting | bytes 1048576

commit v4 on v2

--- a/solution.py
+++ b/solution.py
@@ -44,7 +44,7 @@
     pieces = nf // TILE
     vocab = table_hbm.shape[0]
     n_tab, vocab_pad, tab_tile = tab.shape
-    rows = ids_ref.shape[1]
+    rows = ids_ref.shape[2]
     toks = n_col * rows
 
     w_copies = [
@@ -166,7 +166,8 @@
         lane = lax.broadcasted_iota(jnp.int32, (rows, 128), 1)
         for d in range(n_col):
             at = (col + d) % n_col
-            local = (ids_ref[c] if d == 0 else idbuf[at, c]) - base - lane
+            line = ids_ref[c] if d == 0 else idbuf[at, c]
+            local = jnp.transpose(jnp.broadcast_to(line, (128, rows))) - base - lane
             for i in range(vocab_pad // 128):
                 hit = jnp.where(local == i * 128, 1.0, 0.0).astype(jnp.bfloat16)
                 onehot[at, :, i * 128:(i + 1) * 128] = hit
@@ -345,7 +346,7 @@
     t4 = n_col * rows // 4
     nq, nf = w_qkv.shape[1], w_gate.shape[1]
     width = 2 * nf + (nq + 2 + 127) // 128 * 128
-    ids = jnp.broadcast_to(token_ids.reshape(chunks, rows, 1), (chunks, rows, 128))
+    ids = token_ids.reshape(chunks, 1, rows)
     tab_tile = 512 if dk % 512 == 0 else 128
     n_tab = dk // tab_tile
     vocab_pad = (vocab_rows + 127) // 128 * 128
@@ -364,7 +365,7 @@
         out_specs=(vmem, vmem),
         scratch_shapes=[
             pltpu.VMEM((n_tab, vocab_pad, tab_tile), bf),
-            pltpu.VMEM((n_col, chunks, rows, 128), jnp.int32),
+            pltpu.VMEM((n_col, chunks, 1, rows), jnp.int32),
             pltpu.VMEM((n_col, rows, vocab_pad), bf),
             pltpu.VMEM((chunks, 4, t4, dk), bf),
             pltpu.VMEM((nq, dk), bf),

time: 83.3 us -> 81.7 us (0.981)
  Pallas kernels: 77.3 us -> 75.8 us
    broadcast_in_dim x2 -> x0, local copies, waits for them, and re-layouts: 1.52 us -> none  [body(): jnp.broadcast_to(token_ids.reshape(chunks, rows, 1), (chunks, rows, 128))]
    pallas_call x1, Pallas kernels: 77.3 us -> 75.8 us  [body(): pl.pallas_call(functools.partial(kernel, n_row, n_col, chunks, width, dk...]
    reshape x0 -> x1, local copies, waits for them, and re-layouts: none -> 1.34 us  [body(): ids = token_ids.reshape(chunks, 1, rows)]
where the time goes in v4:
time: 81.7 us; the launch traced here: 81.4 us
  Pallas kernels  75.8 us (93%)
  local copies, waits for them, and re-layouts  4.98 us (6%)
    pallas_call x1, Pallas kernels, body(): pl.pallas_call(functools.partial(kernel, n_row, n_col, chunks, width, dk...  75.8 us
    unnamed x2, local copies, waits for them, and re-layouts  3.64 us

profile of v4, /device:TPU:0, one launch (start us, length us, event | category | flops | bytes accessed | tf_op | source)
XLA Modules:
  0.0 81.4 jit_solution(2469238562758448233)
XLA Ops:
  0.6 1.3 %reshape.16.ids_ref = s32[4,1,64]{2,1,0:T(1,128)} reshape(s32[256]{0:T(256)} %param.6) | data formatting | bytes 2048 | tf_op jit(solution)/shard_map/reshape | solution.py:349
  2.0 75.8 %shard_map.77 = (bf16[4,64,448]{2,1,0:T(8,128)(2,1)}, bf16[4,64,1024]{2,1,0:T(8,128)(2,1)}) custom-call(s32[4,1,64]{2,1,0:T(1,128)} %reshape.16.ids_ref, bf16[3160,2560]{1,0:T(8,128)(2,1)} %table_hbm.1, f32[1,5120]{1,0:T(1,128)} %bitcast.7, bf16[448,2560]{1,0:T(8,128)(2,1)} %bitcast.4, bf16[2560,1024]{1,0:T(8,128)(2,1)} %wg_hbm.1, bf16[2560,1024]{1,0:T(8,128)(2,1)} %wu_hbm.1), custom_call_target="tpu_custom_call" | custom-call | tf_op jit(solution)/shard_map/pallas_call | solution.py:358
  77.7 1.8 %copy.8 = bf16[256,448]{0,1:T(8,128)(2,1)} copy(bf16[256,448]{1,0:T(8,128)(2,1)} %bitcast.6) | data formatting | bytes 458752
  79.5 1.9 %copy.10 = bf16[256,1024]{1,0:T(8,128)(2,1)} copy(bf16[256,1024]{1,0:T(8,128)(2,1)} %bitcast.5) | data formatting | bytes 1048576
